TPU v7x, 32 devices: a whole 2x2x4 slice. The times are simulated.
32 devices in a mesh: fsdp: 4 (over y, x), grp: 8 (over z, core).
Axes of the slice: x: 2, y: 2, z: 4, core: 2. Of those that a mesh axis runs over, the one named last changes fastest.
Arguments:
- grad_out: bfloat16 [32, 512, 512], P(('fsdp', 'grp')), may hold values from -6 to 6
- pre_first: bfloat16 [32, 512, 512], P(('fsdp', 'grp')), may hold values from -8 to 8
- pre_second: bfloat16 [32, 512, 512], P(('fsdp', 'grp')), may hold values from -8 to 8
- conv_first: bfloat16 [3, 512, 512], P(None, 'fsdp'), may hold values from -0.15625 to 0.15625
- conv_second: bfloat16 [3, 512, 512], P(None, 'fsdp'), may hold values from -0.15625 to 0.15625
- lengths: int32 [32], P(('fsdp', 'grp')), may hold values from 64 to 512
- item_ids: int32 [16384], P('grp'), may hold values from 0 to 8191
- owners: int32 [512, 1], P('grp'), may hold values from 0 to 7; in each aligned block of 64 rows (0 to 63, 64 to 127, ...) at most 16 rows name the same one
Outputs:
- table_grad: float32 [512, 65536], P('fsdp', 'grp')
Inputs may be any that keep to these rules, and one draw needn't show every extreme that they name: `owners`: among the blocks of one group, no owner is named by more than 16 blocks, a bound that some block reaches.
All inputs are finite; a program needn't handle non-finite values.
Results may differ from a plain program's by a relative error of at most 0.0037.
Values may be sent and summed in bfloat16 or wider, within the bound.
A program may use at most 64 MiB of HBM per device.

v0:
```python
import jax
import jax.numpy as jnp
from jax import lax
from jax.sharding import PartitionSpec as P

BLK = 32
ROWS_OWN = 8192


def layer_back(gradient, pre_acts, live_rows, dilation, product):
    seq_len = gradient.shape[0]
    pre_float = pre_acts.astype(jnp.float32)
    sig_val = jax.nn.sigmoid(pre_float)
    deltas = (gradient * sig_val * (1.0 + pre_float * (1.0 - sig_val))).astype(jnp.bfloat16)
    padded = jnp.pad(deltas, ((dilation, dilation), (0, 0)))
    tap_rows = jnp.stack(
        [
            padded[2 * dilation : 2 * dilation + seq_len],
            padded[dilation : dilation + seq_len],
            padded[0:seq_len],
        ]
    )
    return gradient + live_rows * product(tap_rows)


def gathered_product(weights):

    def apply_taps(tap_rows):
        return jnp.einsum(
            "ktd,kpd->tp",
            tap_rows,
            lax.all_gather(weights, "fsdp", axis=1, tiled=True),
            preferred_element_type=jnp.float32,
        )

    return apply_taps


def body(grad_out, pre_first, pre_second, conv_first, conv_second, lengths, item_ids, owners):
    seq_len = grad_out.shape[1]
    positions = jnp.arange(seq_len, dtype=jnp.int32)
    live_rows = (positions < lengths[0]).astype(jnp.float32)[:, None]
    gradient = grad_out[0].astype(jnp.float32)
    gradient = layer_back(gradient, pre_second[0], live_rows, 2, gathered_product(conv_second))
    gradient = layer_back(gradient, pre_first[0], live_rows, 1, gathered_product(conv_first))
    row_grad = (live_rows * gradient).astype(jnp.bfloat16)
    group_cols = lax.all_to_all(row_grad.T, "fsdp", split_axis=0, concat_axis=1, tiled=True)
    feat_cols = group_cols.shape[0]
    owner_count = lax.axis_size("grp")
    blocks = owners.shape[0]
    slot_cap = max(2, 2 * blocks // owner_count)
    block_dest = owners[:, 0]
    dest_hits = (block_dest[:, None] == jnp.arange(owner_count, dtype=jnp.int32)[None, :]).astype(
        jnp.int32
    )
    earlier = jnp.cumsum(dest_hits, axis=0) - dest_hits
    block_rank = jnp.sum(dest_hits * earlier, axis=1)
    slot_index = block_dest * slot_cap + block_rank
    select_int = (
        slot_index[:, None] == jnp.arange(owner_count * slot_cap, dtype=jnp.int32)[None, :]
    ).astype(jnp.int32)
    select_int = select_int.reshape(blocks, owner_count, slot_cap)
    select_map = select_int.astype(jnp.bfloat16)
    block_cols = group_cols.reshape(feat_cols, blocks, BLK)
    send_rows = jnp.einsum(
        "cbr,bos->ocsr", block_cols, select_map, preferred_element_type=jnp.float32
    )
    send_rows = send_rows.astype(jnp.bfloat16).reshape(owner_count, feat_cols, slot_cap * BLK)
    shifted_ids = item_ids.reshape(blocks, BLK) + 1
    send_ids = jnp.einsum("br,bos->osr", shifted_ids, select_int) - 1
    send_ids = send_ids.reshape(owner_count, slot_cap * BLK)
    recv_rows, recv_ids = (
        lax.all_to_all(send_rows, "grp", split_axis=0, concat_axis=0, tiled=True),
        lax.all_to_all(send_ids, "grp", split_axis=0, concat_axis=0, tiled=True),
    )
    flat_rows = jnp.transpose(recv_rows, (0, 2, 1)).reshape(-1, feat_cols).astype(jnp.float32)
    safe_ids = jnp.where(recv_ids < 0, ROWS_OWN, recv_ids).reshape(-1)
    summed = jax.ops.segment_sum(flat_rows, safe_ids, num_segments=ROWS_OWN + 1)
    return summed[:ROWS_OWN].T


def solution(mesh):
    placed = (
        P(("fsdp", "grp"), None, None),
        P(("fsdp", "grp"), None, None),
        P(("fsdp", "grp"), None, None),
        P(None, "fsdp", None),
        P(None, "fsdp", None),
        P(("fsdp", "grp")),
        P("grp"),
        P("grp", None),
    )
    return jax.shard_map(
        body, mesh=mesh, in_specs=placed, out_specs=P("fsdp", "grp"), check_vma=False
    )
```

profile of v0, /device:TPU:1, one launch (start us, length us, event | category | flops | bytes accessed | tf_op | source)
XLA Modules:
  0.0 176.0 jit_solution(7663716986740653124)
XLA Ops:
  6.5 0.7 all-gather.3.cloned.1.call-update
  7.3 0.0 all-gather.5.cloned.1.call-start
  7.3 0.7 all-gather.5.cloned.1.call-update
  8.7 0.7 fusion.74
  9.4 0.1 reduce_window_sum.11
  9.5 0.8 select_reduce_fusion
  10.3 0.0 copy-start.1
  10.4 1.7 fusion.46
  12.1 0.0 copy-start.4
  12.1 0.2 slice_bitcast_fusion.4
  12.4 0.5 fusion.48
  12.8 29.1 %all-gather.3.cloned.1.call-done = bf16[3,512,512]{2,1,0:T(8,128)(2,1)} async-done(((bf16[3,128,512]{2,1,0:T(8,128)(2,1)}), bf16[3,512,512]{2,1,0:T(8,128)(2,1)}) %all-gather.3.cloned.1.call-update) | async-done | bytes 1572880 | tf_op jit(solution)/shard_map/all_gather | solution.py:32
  42.0 3.7 %fusion.54 = (bf16[512,512]{1,0:T(8,128)(2,1)S(1)}, f32[512,512]{1,0:T(8,128)}) fusion(bf16[1,512,512]{2,1,0:T(8,128)(2,1)S(1)} %copy-done.4, bf16[3,512,512]{2,1,0:T(8,128)(2,1)} %all-gather.3.cloned.1.call-done, bf16[1,512,512]{2,1,0:T(8,128)(2,1)S(1)} %get-tuple-element.8, bf16[1,512,512]{2,1,0:T(8,128)(2,1)S(1)} %fusion.48, ...), kind=kOutput, calls=%fused_computation.47 | convolution fusion | flops 810287104 | bytes 5769216 | tf_op jit(solution)/shard_map/ktd,kpd->tp/dot_general | solution.py:29
  45.6 0.2 slice_bitcast_fusion.2
  45.8 28.8 %all-gather.5.cloned.1.call-done = bf16[3,512,512]{2,1,0:T(8,128)(2,1)} async-done(((bf16[3,128,512]{2,1,0:T(8,128)(2,1)}), bf16[3,512,512]{2,1,0:T(8,128)(2,1)}) %all-gather.5.cloned.1.call-update) | async-done | bytes 1572880 | tf_op jit(solution)/shard_map/all_gather | solution.py:32
  74.7 2.4 %fusion.42 = bf16[64,4,8,128]{3,2,1,0:T(8,128)(2,1)S(1)} fusion(f32[512,512]{1,0:T(8,128)S(1)} %copy-done.5, bf16[3,512,512]{2,1,0:T(8,128)(2,1)} %all-gather.5.cloned.1.call-done, bf16[1,512,512]{2,1,0:T(8,128)(2,1)S(1)} %get-tuple-element.6, bf16[1,512,512]{2,1,0:T(8,128)(2,1)S(1)} %bitcast.101, bf16[1,512,512]{2,1,0:T(8,128)(2,1)S(1)} %get-tuple-element.5, ...), kind=kOutput, calls=%fused_computation.36 | convolution fusion | flops 807927808 | bytes 4720640 | tf_op jit(solution)/shard_map/ktd,kpd->tp/dot_general | solution.py:29
  77.1 0.9 copy.34
  78.0 3.5 %all-to-all-start.1 = ((bf16[4,128,512]{1,2,0:T(8,128)(2,1)}), bf16[4,128,512]{1,2,0:T(8,128)(2,1)S(1)}, u32[]{:S(2)}, u32[]{:S(2)}) async-start(bf16[4,128,512]{1,2,0:T(8,128)(2,1)} %bitcast.97), calls=%async_computation.1 | async-start | bytes 1048576 | tf_op jit(solution)/shard_map/all_to_all | solution.py:47
  81.5 0.1 add.52
  81.6 0.2 convolution_add_fusion
  81.8 0.7 all_to_all.30
  82.5 6.3 %all-to-all-done.1 = bf16[4,128,512]{1,2,0:T(8,128)(2,1)S(1)} async-done(((bf16[4,128,512]{1,2,0:T(8,128)(2,1)}), bf16[4,128,512]{1,2,0:T(8,128)(2,1)S(1)}, u32[]{:S(2)}, u32[]{:S(2)}) %all-to-all-start.1) | async-done | bytes 524320 | tf_op jit(solution)/shard_map/all_to_all | solution.py:47
  88.8 6.2 %all-to-all-start = ((s32[8,1,512]{2,1,0:T(1,128)}), s32[8,1,512]{2,1,0:T(1,128)S(1)}, u32[]{:S(2)}, u32[]{:S(2)}) async-start(s32[8,1,512]{2,1,0:T(1,128)} %all_to_all.30), calls=%async_computation | async-start | bytes 32768 | tf_op jit(solution)/shard_map/all_to_all | solution.py:74
  95.0 0.5 fusion.14
  95.5 1.2 copy.21
  96.7 3.2 %all-to-all-done = s32[8,1,512]{2,1,0:T(1,128)S(1)} async-done(((s32[8,1,512]{2,1,0:T(1,128)}), s32[8,1,512]{2,1,0:T(1,128)S(1)}, u32[]{:S(2)}, u32[]{:S(2)}) %all-to-all-start) | async-done | bytes 16416 | tf_op jit(solution)/shard_map/all_to_all | solution.py:74
  99.9 4.2 %all-to-all-start.2 = ((bf16[8,128,512]{1,2,0:T(8,128)(2,1)}), bf16[8,128,512]{1,2,0:T(8,128)(2,1)S(1)}, u32[]{:S(2)}, u32[]{:S(2)}) async-start(bf16[8,128,512]{1,2,0:T(8,128)(2,1)} %bitcast.25), calls=%async_computation.2 | async-start | bytes 2097152 | tf_op jit(solution)/shard_map/all_to_all | solution.py:73
  104.2 25.6 %all-to-all-done.2 = bf16[8,128,512]{1,2,0:T(8,128)(2,1)S(1)} async-done(((bf16[8,128,512]{1,2,0:T(8,128)(2,1)}), bf16[8,128,512]{1,2,0:T(8,128)(2,1)S(1)}, u32[]{:S(2)}, u32[]{:S(2)}) %all-to-all-start.2) | async-done | bytes 1048608 | tf_op jit(solution)/shard_map/all_to_all | solution.py:73
  129.8 0.1 convert_element_type.105
  129.9 29.2 %scatter_custom_fusion = f32[8193,128]{1,0:T(8,128)} fusion(s32[4096]{0:T(1024)S(1)} %bitcast.103, f32[4096,128]{1,0:T(8,128)S(1)} %bitcast.99, f32[]{:T(128)} %constant.8.clone.1), kind=kCustom, calls=%fused_computation.2 | custom fusion | flops 524288 | bytes 4194820 | tf_op jit(solution)/shard_map/scatter-add | solution.py:78
  159.1 4.4 %slice_bitcast_fusion = f32[128,8192]{0,1:T(8,128)} fusion(f32[8193,128]{1,0:T(8,128)} %scatter_custom_fusion), kind=kLoop, calls=%fused_computation.1 | loop fusion | bytes 8388608 | tf_op jit(solution)/shard_map/transpose | solution.py:79
  163.5 5.6 %copy.22 = f32[128,8192]{1,0:T(8,128)} copy(f32[128,8192]{0,1:T(8,128)} %slice_bitcast_fusion) | data formatting | bytes 8388608 | tf_op jit(solution)/shard_map/transpose | solution.py:79
  (16 shorter events, 0.1 us)
Async XLA Ops:
  6.5 35.4 %all-gather.3.cloned.1.call-start = ((), (), s32[]{:S(2)}) async-start(), calls=%async_computation.3 | async-start | bytes 1966080 | tf_op jit(solution)/shard_map/all_gather | solution.py:32
  7.3 67.4 %all-gather.5.cloned.1.call-start = ((), (), s32[]{:S(2)}) async-start(), calls=%async_computation.4 | async-start | bytes 1966080 | tf_op jit(solution)/shard_map/all_gather | solution.py:32
  10.3 2.0 %copy-start.2 = (s32[2048]{0:T(1024)S(1)}, s32[2048]{0:T(1024)}, u32[]{:S(2)}) copy-start(s32[2048]{0:T(1024)} %param.14) | copy-start | bytes 24580
  10.3 2.0 %copy-start = (bf16[1,512,512]{2,1,0:T(8,128)(2,1)S(1)}, bf16[1,512,512]{2,1,0:T(8,128)(2,1)}, u32[]{:S(2)}) copy-start(bf16[1,512,512]{2,1,0:T(8,128)(2,1)} %param.10) | copy-start | bytes 1572868
  10.3 2.0 %copy-start.1 = (bf16[1,512,512]{2,1,0:T(8,128)(2,1)S(1)}, bf16[1,512,512]{2,1,0:T(8,128)(2,1)}, u32[]{:S(2)}) copy-start(bf16[1,512,512]{2,1,0:T(8,128)(2,1)} %param.8) | copy-start | bytes 1572868
  12.1 29.9 %copy-start.4 = (bf16[1,512,512]{2,1,0:T(8,128)(2,1)S(1)}, bf16[1,512,512]{2,1,0:T(8,128)(2,1)}, u32[]{:S(2)}) copy-start(bf16[1,512,512]{2,1,0:T(8,128)(2,1)} %param.9) | copy-start | bytes 1572868
  45.6 29.0 %copy-start.5 = (f32[512,512]{1,0:T(8,128)S(1)}, f32[512,512]{1,0:T(8,128)}, u32[]{:S(2)}) copy-start(f32[512,512]{1,0:T(8,128)} %get-tuple-element.10) | copy-start | bytes 3145732
  77.1 4.4 %copy-start.3 = (s32[64,1]{0,1:T(1,128)S(1)}, s32[64,1]{0,1:T(1,128)}, u32[]{:S(2)}) copy-start(s32[64,1]{0,1:T(1,128)} %param.15) | copy-start | bytes 772
  78.0 10.8 %all-to-all-start.1 = ((bf16[4,128,512]{1,2,0:T(8,128)(2,1)}), bf16[4,128,512]{1,2,0:T(8,128)(2,1)S(1)}, u32[]{:S(2)}, u32[]{:S(2)}) async-start(bf16[4,128,512]{1,2,0:T(8,128)(2,1)} %bitcast.97), calls=%async_computation.1 | async-start | bytes 1048576 | tf_op jit(solution)/shard_map/all_to_all | solution.py:47
  88.8 11.2 %all-to-all-start = ((s32[8,1,512]{2,1,0:T(1,128)}), s32[8,1,512]{2,1,0:T(1,128)S(1)}, u32[]{:S(2)}, u32[]{:S(2)}) async-start(s32[8,1,512]{2,1,0:T(1,128)} %all_to_all.30), calls=%async_computation | async-start | bytes 32768 | tf_op jit(solution)/shard_map/all_to_all | solution.py:74
  99.9 29.8 %all-to-all-start.2 = ((bf16[8,128,512]{1,2,0:T(8,128)(2,1)}), bf16[8,128,512]{1,2,0:T(8,128)(2,1)S(1)}, u32[]{:S(2)}, u32[]{:S(2)}) async-start(bf16[8,128,512]{1,2,0:T(8,128)(2,1)} %bitcast.25), calls=%async_computation.2 | async-start | bytes 2097152 | tf_op jit(solution)/shard_map/all_to_all | solution.py:73
Sparse Core Ops, SparseCore 0:
  9.2 32.7 all-gather.2
  43.8 30.8 all-gather.4
where the time goes:
time: 177 us; the launch traced here: 176 us
  waiting for transfers between devices  94.4 us (53%)
  other arithmetic  33.2 us (19%)
  between operations  14.2 us (8%)
  starting transfers between devices  13.9 us (8%)
  local copies, waits for them, and re-layouts  13.4 us (8%)
  matrix products  6.82 us (4%)
    all_gather x2, waiting for transfers between devices, apply_taps(): lax.all_gather(weights, 'fsdp', axis=1, tiled=True)  58 us
    scatter-add x1, other arithmetic, body(): summed = jax.ops.segment_sum(flat_rows, safe_ids, num_segments=ROWS_OWN + 1)  29.2 us
    all_to_all x1, waiting for transfers between devices, body(): lax.all_to_all(send_rows, 'grp', split_axis=0, concat_axis=0, tiled=True)  25.6 us
    transpose x2, local copies, waits for them, and re-layouts, body(): return summed[:ROWS_OWN].T  10 us
    all_to_all x1, waiting for transfers between devices, body(): lax.all_to_all(row_grad.T, 'fsdp', split_axis=0, concat_axis=1, tiled=True)  6.27 us
    all_to_all x1, starting transfers between devices, body(): lax.all_to_all(send_ids, 'grp', split_axis=0, concat_axis=0, tiled=True)  6.23 us
    dot_general x2, matrix products, apply_taps(): jnp.einsum('ktd,kpd->tp', tap_rows, lax.all_gather(weights, 'fsdp', axis=...  6.09 us
    all_to_all x1, starting transfers between devices, body(): lax.all_to_all(send_rows, 'grp', split_axis=0, concat_axis=0, tiled=True)  4.19 us
  transfers between devices with their start and end apart: 5, of which 5 were waited for; matrix products, arithmetic and copies ran while one was open for 6% of the time, Pallas kernels for 0%

commit v1 on v0

--- a/solution.py
+++ b/solution.py
@@ -1,10 +1,427 @@
+import functools
+
 import jax
 import jax.numpy as jnp
 from jax import lax
+from jax.experimental import pallas as pl
+from jax.experimental.pallas import tpu as pltpu
 from jax.sharding import PartitionSpec as P
 
+MESH = pl.DeviceIdType.MESH
 BLK = 32
 ROWS_OWN = 8192
+PAD = 8
+TABLES = 4
+
+
+def flip(index, mask):
+    out = 0
+    for bit in range(6):
+        have = (index // (1 << bit)) % 2
+        out = out + ((1 - have) if (mask >> bit) & 1 else have) * (1 << bit)
+    return out
+
+
+def plan_kernel(slot_cap, own_ref, ids_ref, src_ref, sid_ref, cnt_ref):
+    blocks = ids_ref.shape[0]
+    slots = sid_ref.shape[0]
+    sid_ref[...] = jnp.full(sid_ref.shape, -1, jnp.int32)
+
+    def clear_src(i, c):
+        src_ref[i] = 0
+        return c
+
+    def clear_cnt(i, c):
+        cnt_ref[i] = 0
+        return c
+
+    lax.fori_loop(0, slots, clear_src, 0)
+    lax.fori_loop(0, slots // slot_cap, clear_cnt, 0)
+
+    def place(b, c):
+        owner = own_ref[b]
+        rank = cnt_ref[owner]
+        cnt_ref[owner] = rank + 1
+        slot = owner * slot_cap + rank
+        src_ref[slot] = b
+        sid_ref[pl.ds(slot, 1), :] = ids_ref[pl.ds(b, 1), :]
+        return c
+
+    lax.fori_loop(0, blocks, place, 0)
+
+
+def exchange_kernel(
+    slot_cap,
+    owner_count,
+    src_ref,
+    len_ref,
+    ids_ref,
+    go_ref,
+    p1_ref,
+    p2_ref,
+    w1_ref,
+    w2_ref,
+    rows_out,
+    ids_out,
+    wfull,
+    pad,
+    dsh,
+    grad,
+    rg,
+    gcols,
+    send,
+    dir_s,
+    dir_r,
+    rel_s,
+    rel_r,
+    fw_s,
+    fw_r,
+    feat_s,
+    feat_r,
+    row_s,
+    row_r,
+    id_s,
+    id_r,
+):
+    f = lax.axis_index("fsdp")
+    g = lax.axis_index("grp")
+    core = g % 2
+    seq = grad.shape[0]
+    width = grad.shape[1]
+    cols = width // 4
+    half = cols // 2
+    quarter = cols // 4
+    fx, fy, fd = flip(f, 1), flip(f, 2), flip(f, 3)
+    mate = flip(g, 1)
+
+    barrier = pltpu.get_barrier_semaphore()
+    for peer in (fx, fy, fd):
+        pl.semaphore_signal(barrier, inc=1, device_id=(peer, g), device_id_type=MESH)
+    for m in range(1, owner_count):
+        pl.semaphore_signal(barrier, inc=1, device_id=(f, flip(g, m)), device_id_type=MESH)
+    pl.semaphore_wait(barrier, 3 + owner_count - 1)
+
+    w_refs = (w2_ref, w1_ref)
+
+    def part(layer, owner, off, rows):
+        return wfull.at[layer, :, pl.ds(pl.multiple_of(owner * cols + off, quarter), rows), :]
+
+    def direct(layer, way, sub):
+        peer = (fx, fy)[way]
+        off = core * half + sub * quarter
+        return pltpu.make_async_remote_copy(
+            src_ref=w_refs[layer].at[:, pl.ds(pl.multiple_of(off, quarter), quarter), :],
+            dst_ref=part(layer, f, off, quarter),
+            send_sem=dir_s.at[layer, way, sub],
+            recv_sem=dir_r.at[layer, way, sub],
+            device_id=(peer, g),
+            device_id_type=MESH,
+        )
+
+    def relay(layer, sub):
+        holder, peer = ((fx, fy), (fy, fx))[sub]
+        place = part(layer, holder, core * half + sub * quarter, quarter)
+        return pltpu.make_async_remote_copy(
+            src_ref=place,
+            dst_ref=place,
+            send_sem=rel_s.at[layer, sub],
+            recv_sem=rel_r.at[layer, sub],
+            device_id=(peer, g),
+            device_id_type=MESH,
+        )
+
+    def forward(layer, which):
+        place = part(layer, (fx, fy, fd)[which], core * half, half)
+        return pltpu.make_async_remote_copy(
+            src_ref=place,
+            dst_ref=place,
+            send_sem=fw_s.at[layer, which],
+            recv_sem=fw_r.at[layer, which],
+            device_id=(f, mate),
+            device_id_type=MESH,
+        )
+
+    directs = [[[direct(l, w, s) for s in range(2)] for w in range(2)] for l in range(2)]
+    relays = [[relay(l, s) for s in range(2)] for l in range(2)]
+    forwards = [[forward(l, i) for i in range(3)] for l in range(2)]
+
+    def start_directs(layer):
+        directs[layer][0][0].start()
+        directs[layer][1][1].start()
+        directs[layer][0][1].start()
+        directs[layer][1][0].start()
+
+    def start_relays(layer):
+        directs[layer][0][0].wait_recv()
+        relays[layer][0].start()
+        directs[layer][1][1].wait_recv()
+        relays[layer][1].start()
+
+    def start_forwards(layer):
+        directs[layer][0][1].wait_recv()
+        forwards[layer][0].start()
+        directs[layer][1][0].wait_recv()
+        forwards[layer][1].start()
+        relays[layer][0].wait_recv()
+        relays[layer][1].wait_recv()
+        forwards[layer][2].start()
+
+    def wait_forwards(layer):
+        for i in range(3):
+            forwards[layer][i].wait_recv()
+
+    start_directs(0)
+
+    id_copies = []
+    for m in range(1, owner_count):
+        dest = flip(g, m)
+        id_copies.append(
+            pltpu.make_async_remote_copy(
+                src_ref=ids_ref.at[pl.ds(pl.multiple_of(dest * slot_cap, slot_cap), slot_cap), :],
+                dst_ref=ids_out.at[pl.ds(pl.multiple_of(g * slot_cap, slot_cap), slot_cap), :],
+                send_sem=id_s.at[m - 1],
+                recv_sem=id_r.at[m - 1],
+                device_id=(f, dest),
+                device_id_type=MESH,
+            )
+        )
+        id_copies[-1].start()
+    own_ids = pl.ds(pl.multiple_of(g * slot_cap, slot_cap), slot_cap)
+    ids_out[own_ids, :] = ids_ref[own_ids, :]
+
+    pad[0:PAD, :] = jnp.zeros((PAD, width), jnp.float32)
+    pad[PAD + seq : 2 * PAD + seq, :] = jnp.zeros((PAD, width), jnp.float32)
+    own_cols = pl.ds(pl.multiple_of(f * cols, cols), cols)
+    wfull[0, :, own_cols, :] = w2_ref[...]
+    wfull[1, :, own_cols, :] = w1_ref[...]
+    step = 64
+
+    def taps(first, pre_ref, dilation):
+        for i in range(seq // step):
+            rows = slice(i * step, (i + 1) * step)
+            z = pre_ref[rows, :].astype(jnp.float32)
+            s = jax.nn.sigmoid(z)
+            grad_rows = first[rows, :].astype(jnp.float32)
+            d = (grad_rows * s * (1.0 + z * (1.0 - s))).astype(jnp.bfloat16)
+            dsh[1, rows, :] = d
+            pad[PAD + i * step : PAD + (i + 1) * step, :] = d.astype(jnp.float32)
+        for i in range(seq // step):
+            rows = slice(i * step, (i + 1) * step)
+            low = PAD + i * step
+            dsh[0, rows, :] = pad[low + dilation : low + dilation + step, :].astype(jnp.bfloat16)
+            dsh[2, rows, :] = pad[low - dilation : low - dilation + step, :].astype(jnp.bfloat16)
+
+    def product(layer, rows, wrows):
+        total = None
+        for k in range(3):
+            one = lax.dot_general(
+                dsh[k, rows, :],
+                wfull[layer, k, wrows, :],
+                (((1,), (1,)), ((), ())),
+                preferred_element_type=jnp.float32,
+            )
+            total = one if total is None else total + one
+        return total
+
+    mrows = seq // 2
+
+    def live_of(i):
+        spots = lax.broadcasted_iota(jnp.int32, (mrows, 1), 0) + i * mrows
+        return (spots < len_ref[0]).astype(jnp.float32)
+
+    taps(go_ref, p2_ref, 2)
+    start_relays(0)
+    start_directs(1)
+    start_forwards(0)
+    wait_forwards(0)
+    for j in range(2):
+        wrows = slice(j * 2 * cols, (j + 1) * 2 * cols)
+        for i in range(2):
+            rows = slice(i * mrows, (i + 1) * mrows)
+            grad[rows, wrows] = go_ref[rows, wrows].astype(jnp.float32) + live_of(i) * product(
+                0, rows, wrows
+            )
+    start_relays(1)
+    taps(grad, p1_ref, 1)
+    start_forwards(1)
+    wait_forwards(1)
+
+    feat_copies = []
+    for n, dest in enumerate((fd, fx, fy, f)):
+        wrows = pl.ds(pl.multiple_of(dest * cols, cols), cols)
+        for i in range(2):
+            rows = slice(i * mrows, (i + 1) * mrows)
+            live = live_of(i)
+            full = grad[rows, wrows] + live * product(1, rows, wrows)
+            full = (live * full).astype(jnp.bfloat16)
+            full = full.reshape(mrows // BLK, BLK, cols)
+            spots = pl.ds(i * (mrows // BLK), mrows // BLK)
+            if n < 3:
+                rg[n, spots] = full
+            else:
+                gcols[pl.ds(f * (seq // BLK) + i * (mrows // BLK), mrows // BLK)] = full
+        if n < 3:
+            copy = pltpu.make_async_remote_copy(
+                src_ref=rg.at[n],
+                dst_ref=gcols.at[pl.ds(f * (seq // BLK), seq // BLK)],
+                send_sem=feat_s.at[n],
+                recv_sem=feat_r.at[n],
+                device_id=(dest, g),
+                device_id_type=MESH,
+            )
+            copy.start()
+            feat_copies.append(copy)
+    for copy in feat_copies:
+        copy.wait()
+
+    order = [m for m in range(owner_count - 1, 0, -1)]
+    order = sorted(order, key=lambda m: -(m // 2))
+    row_copies = []
+    for m in order:
+        dest = flip(g, m)
+
+        def pick(s, c, dest=dest, m=m):
+            src = src_ref[dest * slot_cap + s]
+            send[m, s] = gcols[src]
+            return c
+
+        lax.fori_loop(0, slot_cap, pick, 0, unroll=True)
+        copy = pltpu.make_async_remote_copy(
+            src_ref=send.at[m],
+            dst_ref=rows_out.at[g],
+            send_sem=row_s.at[m - 1],
+            recv_sem=row_r.at[m - 1],
+            device_id=(f, dest),
+            device_id_type=MESH,
+        )
+        copy.start()
+        row_copies.append(copy)
+
+    def pick_own(s, c):
+        src = src_ref[g * slot_cap + s]
+        rows_out[g, s] = gcols[src]
+        return c
+
+    lax.fori_loop(0, slot_cap, pick_own, 0, unroll=True)
+    for copy in id_copies + row_copies:
+        copy.wait()
+    for l in range(2):
+        for w in range(2):
+            for s in range(2):
+                directs[l][w][s].wait_send()
+        for s in range(2):
+            relays[l][s].wait_send()
+        for i in range(3):
+            forwards[l][i].wait_send()
+
+
+def table_kernel(ids_ref, rows_ref, out_ref, wide, *tables):
+    slots = ids_ref.shape[0]
+    chunk = out_ref.shape[1]
+
+    @pl.when(pl.program_id(0) == 0)
+    def _():
+        def clear(i, c):
+            spot = pl.ds(pl.multiple_of(i * 128, 128), 128)
+            for table in tables:
+                table[spot, :] = jnp.zeros((128, table.shape[1]), jnp.float32)
+            return c
+
+        lax.fori_loop(0, ROWS_OWN // 128, clear, 0)
+
+        def add_slot(s, c):
+            @pl.when(ids_ref[s, 0] >= 0)
+            def _():
+                base = pl.multiple_of(s * BLK, BLK)
+                wide[...] = rows_ref[pl.ds(base, BLK), :].astype(jnp.float32)
+                for r in range(0, BLK, TABLES):
+                    spots = [pl.ds(ids_ref[s, r + q], 1) for q in range(TABLES)]
+                    olds = [tables[q][spots[q], :] for q in range(TABLES)]
+                    for q in range(TABLES):
+                        tables[q][spots[q], :] = olds[q] + wide[r + q : r + q + 1, :]
+
+            return c
+
+        lax.fori_loop(0, slots, add_slot, 0)
+
+    spot = pl.ds(pl.multiple_of(pl.program_id(0) * chunk, chunk), chunk)
+    total = tables[0][spot, :]
+    for table in tables[1:]:
+        total = total + table[spot, :]
+    out_ref[...] = total.T
+
+
+def fused_body(grad_out, pre_first, pre_second, conv_first, conv_second, lengths, item_ids, owners):
+    seq, width = grad_out.shape[1:]
+    cols = conv_first.shape[1]
+    owner_count = lax.axis_size("grp")
+    blocks = owners.shape[0]
+    slot_cap = max(2, 2 * blocks // owner_count)
+    slots = owner_count * slot_cap
+    smem = pl.BlockSpec(memory_space=pltpu.SMEM)
+    vmem = pl.BlockSpec(memory_space=pltpu.VMEM)
+    source, send_ids = pl.pallas_call(
+        functools.partial(plan_kernel, slot_cap),
+        out_shape=(
+            jax.ShapeDtypeStruct((slots,), jnp.int32),
+            jax.ShapeDtypeStruct((slots, BLK), jnp.int32),
+        ),
+        in_specs=[smem, vmem],
+        out_specs=(smem, vmem),
+        scratch_shapes=[pltpu.SMEM((owner_count,), jnp.int32)],
+    )(owners.reshape(blocks), item_ids.reshape(blocks, BLK))
+    dma = pltpu.SemaphoreType.DMA
+    bf16 = jnp.bfloat16
+    rows, ids = pl.pallas_call(
+        functools.partial(exchange_kernel, slot_cap, owner_count),
+        out_shape=(
+            jax.ShapeDtypeStruct((owner_count, slot_cap, BLK, cols), bf16),
+            jax.ShapeDtypeStruct((slots, BLK), jnp.int32),
+        ),
+        in_specs=[smem, smem] + [vmem] * 6,
+        out_specs=(vmem, vmem),
+        scratch_shapes=[
+            pltpu.VMEM((2, 3, width, width), bf16),
+            pltpu.VMEM((seq + 2 * PAD, width), jnp.float32),
+            pltpu.VMEM((3, seq, width), bf16),
+            pltpu.VMEM((seq, width), jnp.float32),
+            pltpu.VMEM((3, seq // BLK, BLK, cols), bf16),
+            pltpu.VMEM((4 * seq // BLK, BLK, cols), bf16),
+            pltpu.VMEM((owner_count, slot_cap, BLK, cols), bf16),
+            dma((2, 2, 2)),
+            dma((2, 2, 2)),
+            dma((2, 2)),
+            dma((2, 2)),
+            dma((2, 3)),
+            dma((2, 3)),
+            dma((3,)),
+            dma((3,)),
+            dma((owner_count - 1,)),
+            dma((owner_count - 1,)),
+            dma((owner_count - 1,)),
+            dma((owner_count - 1,)),
+        ],
+        compiler_params=pltpu.CompilerParams(collective_id=0, has_side_effects=True),
+    )(
+        source,
+        lengths,
+        send_ids,
+        grad_out.reshape(seq, width),
+        pre_first.reshape(seq, width),
+        pre_second.reshape(seq, width),
+        conv_first,
+        conv_second,
+    )
+    chunk = 512
+    return pl.pallas_call(
+        table_kernel,
+        grid=(ROWS_OWN // chunk,),
+        out_shape=jax.ShapeDtypeStruct((cols, ROWS_OWN), jnp.float32),
+        in_specs=[smem, pl.BlockSpec((slots * BLK, cols), lambda i: (0, 0))],
+        out_specs=pl.BlockSpec((cols, chunk), lambda i: (0, i)),
+        scratch_shapes=[pltpu.VMEM((BLK, cols), jnp.float32)]
+        + [pltpu.VMEM((ROWS_OWN, cols), jnp.float32)] * TABLES,
+    )(ids, rows.reshape(slots * BLK, cols))
 
 
 def layer_back(gradient, pre_acts, live_rows, dilation, product):
@@ -80,6 +497,7 @@
 
 
 def solution(mesh):
+    fused = mesh.shape["fsdp"] == 4 and mesh.shape["grp"] == 8
     placed = (
         P(("fsdp", "grp"), None, None),
         P(("fsdp", "grp"), None, None),
@@ -91,5 +509,5 @@
         P("grp", None),
     )
     return jax.shard_map(
-        body, mesh=mesh, in_specs=placed, out_specs=P("fsdp", "grp"), check_vma=False
-    )
+        fused_body if fused else body, mesh=mesh, in_specs=placed, out_specs=P("fsdp", "grp"), check_vma=False
+    )

time: 177 us -> 78.6 us (0.44)
  waiting for transfers between devices: 94.4 us -> 0 us
  Pallas kernels: 0 us -> 76.7 us
  other arithmetic: 33.2 us -> 0 us
  starting transfers between devices: 13.9 us -> 0 us
  between operations: 14.2 us -> 0.67 us
  local copies, waits for them, and re-layouts: 13.4 us -> 1.37 us
  matrix products: 6.82 us -> 0 us
    pallas_call x0 -> x3, Pallas kernels: none -> 76.7 us  [the longest x1 57.7 us: fused_body(): pl.pallas_call(functools.partial(exchange_kernel, slot_cap, owner_count),...]
    all_gather x2 -> x0, waiting for transfers between devices: 58 us -> none  [apply_taps(): lax.all_gather(weights, 'fsdp', axis=1, tiled=True)]
    all_to_all x3 -> x0, waiting for transfers between devices: 35.1 us -> none  [the longest x1 25.6 us: body(): lax.all_to_all(send_rows, 'grp', split_axis=0, concat_axis=0, tiled=True)]
    scatter-add x1 -> x0, other arithmetic: 29.2 us -> none  [body(): summed = jax.ops.segment_sum(flat_rows, safe_ids, num_segments=ROWS_OWN + 1)]
    all_to_all x3 -> x0, starting transfers between devices: 13.9 us -> none  [the longest x1 6.23 us: body(): lax.all_to_all(send_ids, 'grp', split_axis=0, concat_axis=0, tiled=True)]
    transpose x2 -> x0, local copies, waits for them, and re-layouts: 10 us -> none  [body(): return summed[:ROWS_OWN].T]
    dot_general x4 -> x0, matrix products: 6.82 us -> none  [the longest x2 6.09 us: apply_taps(): jnp.einsum('ktd,kpd->tp', tap_rows, lax.all_gather(weights, 'fsdp', axis=...]
    convert_element_type x5 -> x0, other arithmetic: 3.05 us -> none  [the longest x2 2.18 us: layer_back(): (gradient * sig_val * (1.0 + pre_float * (1.0 - sig_val))).astype(jnp.bfl...]
  transfers between devices with their start and end apart: 5 -> 0, of which waited for: 5 -> 0; matrix products, arithmetic and copies ran while one was open for 6% -> 0% of each run, Pallas kernels for 0% -> 0%
where the time goes in v1:
time: 78.6 us; the launch traced here: 78.7 us
  Pallas kernels  76.7 us (98%)
  local copies, waits for them, and re-layouts  1.37 us (2%)
    pallas_call x1, Pallas kernels, fused_body(): pl.pallas_call(functools.partial(exchange_kernel, slot_cap, owner_count),...  57.7 us
    pallas_call x1, Pallas kernels, fused_body(): pl.pallas_call(table_kernel, grid=(ROWS_OWN // chunk,), out_shape=jax.Sha...  15.8 us
    pallas_call x1, Pallas kernels, fused_body(): pl.pallas_call(functools.partial(plan_kernel, slot_cap), out_shape=(jax.S...  3.13 us

profile of v1, /device:TPU:1, one launch (start us, length us, event | category | flops | bytes accessed | tf_op | source)
XLA Modules:
  0.0 78.7 jit_solution(13133128359697040209)
XLA Ops:
  0.7 1.4 %reshape.19.ids_ref = s32[64,32]{1,0:T(8,128)} reshape(s32[2048]{0:T(1024)} %param.14) | data formatting | bytes 16384 | tf_op jit(solution)/shard_map/reshape | solution.py:372
  2.0 3.1 %shard_map.82 = (s32[128]{0:T(128)}, s32[128,32]{1,0:T(8,128)}) custom-call(s32[64]{0:T(128)} %bitcast.9, s32[64,32]{1,0:T(8,128)} %reshape.19.ids_ref), custom_call_target="tpu_custom_call" | custom-call | tf_op jit(solution)/shard_map/pallas_call | solution.py:363
  5.2 57.7 %shard_map.83 = (bf16[8,16,32,128]{3,2,1,0:T(8,128)(2,1)}, s32[128,32]{1,0:T(8,128)}) custom-call(s32[128]{0:T(128)} %get-tuple-element.9.src_ref, s32[1]{0:T(128)S(6)} %copy.9.len_ref, s32[128,32]{1,0:T(8,128)} %get-tuple-element.10.ids_ref, bf16[512,512]{1,0:T(8,128)(2,1)} %bitcast.6, bf16[512,512]{1,0:T(8,128)(2,1)} %bitcast.7, bf16[512,512]{1,0:T(8,128)(2,1)} %bitcast.8, ...), custom_call_target="tpu_custom_call" | custom-call | tf_op jit(solution)/shard_map/pallas_call | solution.py:375
  62.9 15.8 %shard_map.84 = f32[128,8192]{1,0:T(8,128)} custom-call(s32[128,32]{1,0:T(8,128)} %get-tuple-element.11.ids_ref, bf16[4096,128]{1,0:T(8,128)(2,1)} %bitcast.5), custom_call_target="tpu_custom_call" | custom-call | tf_op jit(solution)/shard_map/pallas_call | solution.py:416

commit v2 on v1

--- a/solution.py
+++ b/solution.py
@@ -22,40 +22,38 @@
     return out
 
 
-def plan_kernel(slot_cap, own_ref, ids_ref, src_ref, sid_ref, cnt_ref):
-    blocks = ids_ref.shape[0]
-    slots = sid_ref.shape[0]
-    sid_ref[...] = jnp.full(sid_ref.shape, -1, jnp.int32)
-
-    def clear_src(i, c):
-        src_ref[i] = 0
-        return c
-
-    def clear_cnt(i, c):
-        cnt_ref[i] = 0
-        return c
-
-    lax.fori_loop(0, slots, clear_src, 0)
-    lax.fori_loop(0, slots // slot_cap, clear_cnt, 0)
-
-    def place(b, c):
-        owner = own_ref[b]
-        rank = cnt_ref[owner]
-        cnt_ref[owner] = rank + 1
-        slot = owner * slot_cap + rank
-        src_ref[slot] = b
-        sid_ref[pl.ds(slot, 1), :] = ids_ref[pl.ds(b, 1), :]
-        return c
-
-    lax.fori_loop(0, blocks, place, 0)
+def slot_plan(slot_cap, slots, own_row, ids_ref):
+    blocks = own_row.shape[1]
+    early = lax.broadcasted_iota(jnp.int32, (blocks, blocks), 0)
+    late = lax.broadcasted_iota(jnp.int32, (blocks, blocks), 1)
+    own_late = jnp.broadcast_to(own_row, (blocks, blocks))
+    own_early = jnp.sum(jnp.where(early == late, own_late, 0), axis=1, keepdims=True)
+    same = (own_early == own_late) & (early < late)
+    rank = jnp.sum(jnp.where(same, 1, 0), axis=0, keepdims=True)
+    slot = own_row * slot_cap + rank
+    hit = slot == lax.broadcasted_iota(jnp.int32, (slots, blocks), 0)
+    index = lax.broadcasted_iota(jnp.int32, (slots, blocks), 1)
+    source = jnp.sum(jnp.where(hit, index, 0), axis=1, keepdims=True)
+    used = jnp.sum(jnp.where(hit, 1, 0), axis=1, keepdims=True)
+    lanes = ids_ref.shape[1]
+    row_of = jnp.broadcast_to(source >> 2, (slots, lanes))
+    lane_of = jnp.broadcast_to(source & 3, (slots, lanes))
+    used = jnp.broadcast_to(used, (slots, lanes))
+    ids = jnp.zeros((slots, lanes), jnp.int32)
+    for r in range(ids_ref.shape[0]):
+        ids = jnp.where(row_of == r, ids_ref[r : r + 1, :], ids)
+    out = ids
+    for q in range(1, 4):
+        out = jnp.where(lane_of == q, pltpu.roll(ids, lanes - q * BLK, 1), out)
+    return jnp.broadcast_to(source, (slots, lanes)), jnp.where(used > 0, out, -1)
 
 
 def exchange_kernel(
     slot_cap,
     owner_count,
-    src_ref,
     len_ref,
-    ids_ref,
+    own_ref,
+    item_ref,
     go_ref,
     p1_ref,
     p2_ref,
@@ -82,6 +80,10 @@
     row_r,
     id_s,
     id_r,
+    ids_ref,
+    src_vmem,
+    src_ref,
+    src_sem,
 ):
     f = lax.axis_index("fsdp")
     g = lax.axis_index("grp")
@@ -99,6 +101,11 @@
         pl.semaphore_signal(barrier, inc=1, device_id=(peer, g), device_id_type=MESH)
     for m in range(1, owner_count):
         pl.semaphore_signal(barrier, inc=1, device_id=(f, flip(g, m)), device_id_type=MESH)
+    pad[0:PAD, :] = jnp.zeros((PAD, width), jnp.float32)
+    pad[PAD + seq : 2 * PAD + seq, :] = jnp.zeros((PAD, width), jnp.float32)
+    own_cols = pl.ds(pl.multiple_of(f * cols, cols), cols)
+    wfull[0, :, own_cols, :] = w2_ref[...]
+    wfull[1, :, own_cols, :] = w1_ref[...]
     pl.semaphore_wait(barrier, 3 + owner_count - 1)
 
     w_refs = (w2_ref, w1_ref)
@@ -157,20 +164,23 @@
         directs[layer][1][1].wait_recv()
         relays[layer][1].start()
 
-    def start_forwards(layer):
+    def start_near_forwards(layer):
         directs[layer][0][1].wait_recv()
         forwards[layer][0].start()
         directs[layer][1][0].wait_recv()
         forwards[layer][1].start()
+
+    def start_far_forward(layer):
         relays[layer][0].wait_recv()
         relays[layer][1].wait_recv()
         forwards[layer][2].start()
 
-    def wait_forwards(layer):
-        for i in range(3):
-            forwards[layer][i].wait_recv()
-
     start_directs(0)
+    source, send_ids = slot_plan(slot_cap, owner_count * slot_cap, own_ref[...], item_ref)
+    ids_ref[...] = send_ids
+    src_vmem[...] = source
+    src_copy = pltpu.make_async_copy(src_vmem, src_ref, src_sem)
+    src_copy.start()
 
     id_copies = []
     for m in range(1, owner_count):
@@ -189,11 +199,6 @@
     own_ids = pl.ds(pl.multiple_of(g * slot_cap, slot_cap), slot_cap)
     ids_out[own_ids, :] = ids_ref[own_ids, :]
 
-    pad[0:PAD, :] = jnp.zeros((PAD, width), jnp.float32)
-    pad[PAD + seq : 2 * PAD + seq, :] = jnp.zeros((PAD, width), jnp.float32)
-    own_cols = pl.ds(pl.multiple_of(f * cols, cols), cols)
-    wfull[0, :, own_cols, :] = w2_ref[...]
-    wfull[1, :, own_cols, :] = w1_ref[...]
     step = 64
 
     def taps(first, pre_ref, dilation):
@@ -232,22 +237,29 @@
     taps(go_ref, p2_ref, 2)
     start_relays(0)
     start_directs(1)
-    start_forwards(0)
-    wait_forwards(0)
-    for j in range(2):
-        wrows = slice(j * 2 * cols, (j + 1) * 2 * cols)
+    start_near_forwards(0)
+    for n, dest in enumerate((f, fx, fy, fd)):
+        if n == 2:
+            start_far_forward(0)
+        if n > 0:
+            forwards[0][n - 1].wait_recv()
+        if n == 3:
+            start_relays(1)
+        wrows = pl.ds(pl.multiple_of(dest * cols, cols), cols)
         for i in range(2):
             rows = slice(i * mrows, (i + 1) * mrows)
             grad[rows, wrows] = go_ref[rows, wrows].astype(jnp.float32) + live_of(i) * product(
                 0, rows, wrows
             )
-    start_relays(1)
     taps(grad, p1_ref, 1)
-    start_forwards(1)
-    wait_forwards(1)
+    start_near_forwards(1)
 
     feat_copies = []
-    for n, dest in enumerate((fd, fx, fy, f)):
+    for n, dest in enumerate((f, fx, fy, fd)):
+        if n == 2:
+            start_far_forward(1)
+        if n > 0:
+            forwards[1][n - 1].wait_recv()
         wrows = pl.ds(pl.multiple_of(dest * cols, cols), cols)
         for i in range(2):
             rows = slice(i * mrows, (i + 1) * mrows)
@@ -256,21 +268,22 @@
             full = (live * full).astype(jnp.bfloat16)
             full = full.reshape(mrows // BLK, BLK, cols)
             spots = pl.ds(i * (mrows // BLK), mrows // BLK)
-            if n < 3:
-                rg[n, spots] = full
+            if n > 0:
+                rg[n - 1, spots] = full
             else:
                 gcols[pl.ds(f * (seq // BLK) + i * (mrows // BLK), mrows // BLK)] = full
-        if n < 3:
+        if n > 0:
             copy = pltpu.make_async_remote_copy(
-                src_ref=rg.at[n],
+                src_ref=rg.at[n - 1],
                 dst_ref=gcols.at[pl.ds(f * (seq // BLK), seq // BLK)],
-                send_sem=feat_s.at[n],
-                recv_sem=feat_r.at[n],
+                send_sem=feat_s.at[n - 1],
+                recv_sem=feat_r.at[n - 1],
                 device_id=(dest, g),
                 device_id_type=MESH,
             )
             copy.start()
             feat_copies.append(copy)
+    src_copy.wait()
     for copy in feat_copies:
         copy.wait()
 
@@ -281,7 +294,7 @@
         dest = flip(g, m)
 
         def pick(s, c, dest=dest, m=m):
-            src = src_ref[dest * slot_cap + s]
+            src = src_ref[dest * slot_cap + s, 0]
             send[m, s] = gcols[src]
             return c
 
@@ -298,7 +311,7 @@
         row_copies.append(copy)
 
     def pick_own(s, c):
-        src = src_ref[g * slot_cap + s]
+        src = src_ref[g * slot_cap + s, 0]
         rows_out[g, s] = gcols[src]
         return c
 
@@ -360,25 +373,15 @@
     slots = owner_count * slot_cap
     smem = pl.BlockSpec(memory_space=pltpu.SMEM)
     vmem = pl.BlockSpec(memory_space=pltpu.VMEM)
-    source, send_ids = pl.pallas_call(
-        functools.partial(plan_kernel, slot_cap),
-        out_shape=(
-            jax.ShapeDtypeStruct((slots,), jnp.int32),
-            jax.ShapeDtypeStruct((slots, BLK), jnp.int32),
-        ),
-        in_specs=[smem, vmem],
-        out_specs=(smem, vmem),
-        scratch_shapes=[pltpu.SMEM((owner_count,), jnp.int32)],
-    )(owners.reshape(blocks), item_ids.reshape(blocks, BLK))
     dma = pltpu.SemaphoreType.DMA
     bf16 = jnp.bfloat16
     rows, ids = pl.pallas_call(
         functools.partial(exchange_kernel, slot_cap, owner_count),
         out_shape=(
             jax.ShapeDtypeStruct((owner_count, slot_cap, BLK, cols), bf16),
-            jax.ShapeDtypeStruct((slots, BLK), jnp.int32),
+            jax.ShapeDtypeStruct((slots, 4 * BLK), jnp.int32),
         ),
-        in_specs=[smem, smem] + [vmem] * 6,
+        in_specs=[smem] + [vmem] * 7,
         out_specs=(vmem, vmem),
         scratch_shapes=[
             pltpu.VMEM((2, 3, width, width), bf16),
@@ -400,19 +403,23 @@
             dma((owner_count - 1,)),
             dma((owner_count - 1,)),
             dma((owner_count - 1,)),
+            pltpu.VMEM((slots, 4 * BLK), jnp.int32),
+            pltpu.VMEM((slots, 4 * BLK), jnp.int32),
+            pltpu.SMEM((slots, 4 * BLK), jnp.int32),
+            dma,
         ],
         compiler_params=pltpu.CompilerParams(collective_id=0, has_side_effects=True),
     )(
-        source,
         lengths,
-        send_ids,
+        owners.reshape(1, blocks),
+        item_ids.reshape(blocks // 4, 4 * BLK),
         grad_out.reshape(seq, width),
         pre_first.reshape(seq, width),
         pre_second.reshape(seq, width),
         conv_first,
         conv_second,
     )
-    chunk = 512
+    chunk = 4096
     return pl.pallas_call(
         table_kernel,
         grid=(ROWS_OWN // chunk,),

time: 78.6 us -> 66 us (0.84); the launches traced: 78.7 us -> 64.7 us
  Pallas kernels: 76.7 us -> 64 us
  local copies, waits for them, and re-layouts: 1.37 us -> 0 us
    pallas_call x1, Pallas kernels: 15.8 us -> 9.43 us  [fused_body(): pl.pallas_call(table_kernel, grid=(ROWS_OWN // chunk,), out_shape=jax.Sha...]
    pallas_call x1, Pallas kernels: 57.7 us -> 54.6 us  [fused_body(): pl.pallas_call(functools.partial(exchange_kernel, slot_cap, owner_count),...]
    pallas_call x1 -> x0, Pallas kernels: 3.13 us -> none  [fused_body(): pl.pallas_call(functools.partial(plan_kernel, slot_cap), out_shape=(jax.S...]
    reshape x1 -> x0, local copies, waits for them, and re-layouts: 1.37 us -> none  [fused_body(): item_ids.reshape(blocks, BLK)]
where the time goes in v2:
time: 66 us; the launch traced here: 64.7 us
  Pallas kernels  64 us (97%)
  between operations  0.66 us (1%)
    pallas_call x1, Pallas kernels, fused_body(): pl.pallas_call(functools.partial(exchange_kernel, slot_cap, owner_count),...  54.6 us
    pallas_call x1, Pallas kernels, fused_body(): pl.pallas_call(table_kernel, grid=(ROWS_OWN // chunk,), out_shape=jax.Sha...  9.43 us

profile of v2, /device:TPU:1, one launch (start us, length us, event | category | flops | bytes accessed | tf_op | source)
XLA Modules:
  0.0 64.7 jit_solution(10150811324309244523)
XLA Ops:
  0.7 54.6 %shard_map.82 = (bf16[8,16,32,128]{3,2,1,0:T(8,128)(2,1)}, s32[128,128]{1,0:T(8,128)}) custom-call(s32[1]{0:T(128)S(6)} %copy.9.len_ref, s32[1,64]{1,0:T(1,128)} %bitcast.11, s32[16,128]{1,0:T(8,128)} %bitcast.10, bf16[512,512]{1,0:T(8,128)(2,1)} %bitcast.7, bf16[512,512]{1,0:T(8,128)(2,1)} %bitcast.8, bf16[512,512]{1,0:T(8,128)(2,1)} %bitcast.9, ...), custom_call_target="tpu_custom_call" | custom-call | tf_op jit(solution)/shard_map/pallas_call | solution.py:378
  55.2 9.4 %shard_map.83 = f32[128,8192]{1,0:T(8,128)} custom-call(s32[128,128]{1,0:T(8,128)} %get-tuple-element.7.ids_ref, bf16[4096,128]{1,0:T(8,128)(2,1)} %bitcast.6), custom_call_target="tpu_custom_call" | custom-call | tf_op jit(solution)/shard_map/pallas_call | solution.py:423

commit v3 on v2

--- a/solution.py
+++ b/solution.py
@@ -72,6 +72,8 @@
     dir_r,
     rel_s,
     rel_r,
+    up_s,
+    up_r,
     fw_s,
     fw_r,
     feat_s,
@@ -95,6 +97,9 @@
     quarter = cols // 4
     fx, fy, fd = flip(f, 1), flip(f, 2), flip(f, 3)
     mate = flip(g, 1)
+    level = flip(g, 2)
+    first_tap = 1 + (g // 2) % 2
+    tap_of = (first_tap, 0, 3 - first_tap)
 
     barrier = pltpu.get_barrier_semaphore()
     for peer in (fx, fy, fd):
@@ -110,70 +115,88 @@
 
     w_refs = (w2_ref, w1_ref)
 
-    def part(layer, owner, off, rows):
-        return wfull.at[layer, :, pl.ds(pl.multiple_of(owner * cols + off, quarter), rows), :]
-
-    def direct(layer, way, sub):
-        peer = (fx, fy)[way]
-        off = core * half + sub * quarter
+    def part(layer, turn, owner, off, rows):
+        spot = pl.ds(pl.multiple_of(owner * cols + off, quarter), rows)
+        return wfull.at[layer, tap_of[turn], spot, :]
+
+    def move(src, dst, send_sem, recv_sem, peer):
         return pltpu.make_async_remote_copy(
-            src_ref=w_refs[layer].at[:, pl.ds(pl.multiple_of(off, quarter), quarter), :],
-            dst_ref=part(layer, f, off, quarter),
-            send_sem=dir_s.at[layer, way, sub],
-            recv_sem=dir_r.at[layer, way, sub],
-            device_id=(peer, g),
+            src_ref=src,
+            dst_ref=dst,
+            send_sem=send_sem,
+            recv_sem=recv_sem,
+            device_id=peer,
             device_id_type=MESH,
         )
 
-    def relay(layer, sub):
+    def direct(layer, turn, way, sub):
+        off = core * half + sub * quarter
+        spot = pl.ds(pl.multiple_of(off, quarter), quarter)
+        at = (layer, turn, way, sub)
+        return move(
+            w_refs[layer].at[tap_of[turn], spot, :],
+            part(layer, turn, f, off, quarter),
+            dir_s.at[at],
+            dir_r.at[at],
+            ((fx, fy)[way], g),
+        )
+
+    def relay(layer, turn, sub):
         holder, peer = ((fx, fy), (fy, fx))[sub]
-        place = part(layer, holder, core * half + sub * quarter, quarter)
-        return pltpu.make_async_remote_copy(
-            src_ref=place,
-            dst_ref=place,
-            send_sem=rel_s.at[layer, sub],
-            recv_sem=rel_r.at[layer, sub],
-            device_id=(peer, g),
-            device_id_type=MESH,
-        )
-
-    def forward(layer, which):
-        place = part(layer, (fx, fy, fd)[which], core * half, half)
-        return pltpu.make_async_remote_copy(
-            src_ref=place,
-            dst_ref=place,
-            send_sem=fw_s.at[layer, which],
-            recv_sem=fw_r.at[layer, which],
-            device_id=(f, mate),
-            device_id_type=MESH,
-        )
-
-    directs = [[[direct(l, w, s) for s in range(2)] for w in range(2)] for l in range(2)]
-    relays = [[relay(l, s) for s in range(2)] for l in range(2)]
-    forwards = [[forward(l, i) for i in range(3)] for l in range(2)]
+        place = part(layer, turn, holder, core * half + sub * quarter, quarter)
+        at = (layer, turn, sub)
+        return move(place, place, rel_s.at[at], rel_r.at[at], (peer, g))
+
+    def along(layer, which):
+        place = part(layer, 0, (fx, fy, fd)[which], core * half, half)
+        at = (layer, which)
+        return move(place, place, up_s.at[at], up_r.at[at], (f, level))
+
+    def forward(layer, turn, which):
+        place = part(layer, turn, (fx, fy, fd)[which], core * half, half)
+        at = (layer, turn, which)
+        return move(place, place, fw_s.at[at], fw_r.at[at], (f, mate))
+
+    two, three = range(2), range(3)
+    directs = [[[[direct(l, t, w, s) for s in two] for w in two] for t in two] for l in two]
+    relays = [[[relay(l, t, s) for s in two] for t in two] for l in two]
+    alongs = [[along(l, i) for i in three] for l in two]
+    forwards = [[[forward(l, t, i) for i in three] for t in three] for l in two]
 
     def start_directs(layer):
-        directs[layer][0][0].start()
-        directs[layer][1][1].start()
-        directs[layer][0][1].start()
-        directs[layer][1][0].start()
-
-    def start_relays(layer):
-        directs[layer][0][0].wait_recv()
-        relays[layer][0].start()
-        directs[layer][1][1].wait_recv()
-        relays[layer][1].start()
-
-    def start_near_forwards(layer):
-        directs[layer][0][1].wait_recv()
-        forwards[layer][0].start()
-        directs[layer][1][0].wait_recv()
-        forwards[layer][1].start()
-
-    def start_far_forward(layer):
-        relays[layer][0].wait_recv()
-        relays[layer][1].wait_recv()
-        forwards[layer][2].start()
+        for turn in two:
+            directs[layer][turn][0][0].start()
+            directs[layer][turn][1][1].start()
+            directs[layer][turn][0][1].start()
+            directs[layer][turn][1][0].start()
+
+    def near(layer, turn):
+        directs[layer][turn][0][0].wait_recv()
+        relays[layer][turn][0].start()
+        directs[layer][turn][1][1].wait_recv()
+        relays[layer][turn][1].start()
+        for way in two:
+            directs[layer][turn][way][1 - way].wait_recv()
+            if turn == 0:
+                alongs[layer][way].start()
+            forwards[layer][turn][way].start()
+
+    def far(layer):
+        for turn in two:
+            relays[layer][turn][0].wait_recv()
+            relays[layer][turn][1].wait_recv()
+            if turn == 0:
+                alongs[layer][2].start()
+            forwards[layer][turn][2].start()
+
+    def upper(layer):
+        for which in three:
+            alongs[layer][which].wait_recv()
+            forwards[layer][2][which].start()
+
+    def shard_ready(layer, which):
+        for turn in three:
+            forwards[layer][turn][which].wait_recv()
 
     start_directs(0)
     source, send_ids = slot_plan(slot_cap, owner_count * slot_cap, own_ref[...], item_ref)
@@ -235,31 +258,33 @@
         return (spots < len_ref[0]).astype(jnp.float32)
 
     taps(go_ref, p2_ref, 2)
-    start_relays(0)
+    near(0, 0)
+    near(0, 1)
     start_directs(1)
-    start_near_forwards(0)
+    far(0)
     for n, dest in enumerate((f, fx, fy, fd)):
-        if n == 2:
-            start_far_forward(0)
+        if n == 1:
+            upper(0)
+            near(1, 0)
+        if n == 3:
+            near(1, 1)
         if n > 0:
-            forwards[0][n - 1].wait_recv()
-        if n == 3:
-            start_relays(1)
+            shard_ready(0, n - 1)
         wrows = pl.ds(pl.multiple_of(dest * cols, cols), cols)
         for i in range(2):
             rows = slice(i * mrows, (i + 1) * mrows)
             grad[rows, wrows] = go_ref[rows, wrows].astype(jnp.float32) + live_of(i) * product(
                 0, rows, wrows
             )
+    far(1)
     taps(grad, p1_ref, 1)
-    start_near_forwards(1)
 
     feat_copies = []
     for n, dest in enumerate((f, fx, fy, fd)):
-        if n == 2:
-            start_far_forward(1)
+        if n == 1:
+            upper(1)
         if n > 0:
-            forwards[1][n - 1].wait_recv()
+            shard_ready(1, n - 1)
         wrows = pl.ds(pl.multiple_of(dest * cols, cols), cols)
         for i in range(2):
             rows = slice(i * mrows, (i + 1) * mrows)
@@ -318,14 +343,17 @@
     lax.fori_loop(0, slot_cap, pick_own, 0, unroll=True)
     for copy in id_copies + row_copies:
         copy.wait()
-    for l in range(2):
-        for w in range(2):
-            for s in range(2):
-                directs[l][w][s].wait_send()
-        for s in range(2):
-            relays[l][s].wait_send()
-        for i in range(3):
-            forwards[l][i].wait_send()
+    for l in two:
+        for t in two:
+            for w in two:
+                for s in two:
+                    directs[l][t][w][s].wait_send()
+            for s in two:
+                relays[l][t][s].wait_send()
+        for i in three:
+            alongs[l][i].wait_send()
+            for t in three:
+                forwards[l][t][i].wait_send()
 
 
 def table_kernel(ids_ref, rows_ref, out_ref, wide, *tables):
@@ -391,12 +419,14 @@
             pltpu.VMEM((3, seq // BLK, BLK, cols), bf16),
             pltpu.VMEM((4 * seq // BLK, BLK, cols), bf16),
             pltpu.VMEM((owner_count, slot_cap, BLK, cols), bf16),
+            dma((2, 2, 2, 2)),
+            dma((2, 2, 2, 2)),
             dma((2, 2, 2)),
             dma((2, 2, 2)),
-            dma((2, 2)),
-            dma((2, 2)),
             dma((2, 3)),
             dma((2, 3)),
+            dma((2, 3, 3)),
+            dma((2, 3, 3)),
             dma((3,)),
             dma((3,)),
             dma((owner_count - 1,)),

time: 66 us -> 68.3 us (1.035)
  Pallas kernels: 64 us -> 66.5 us
    pallas_call x1, Pallas kernels: 54.6 us -> 57.1 us  [fused_body(): pl.pallas_call(functools.partial(exchange_kernel, slot_cap, owner_count),...]
where the time goes in v3:
time: 68.3 us; the launch traced here: 67.2 us
  Pallas kernels  66.5 us (97%)
    pallas_call x1, Pallas kernels, fused_body(): pl.pallas_call(functools.partial(exchange_kernel, slot_cap, owner_count),...  57.1 us
    pallas_call x1, Pallas kernels, fused_body(): pl.pallas_call(table_kernel, grid=(ROWS_OWN // chunk,), out_shape=jax.Sha...  9.43 us

profile of v3, /device:TPU:1, one launch (start us, length us, event | category | flops | bytes accessed | tf_op | source)
XLA Modules:
  0.0 67.2 jit_solution(16627003818981417955)
XLA Ops:
  0.7 57.1 %shard_map.82 = (bf16[8,16,32,128]{3,2,1,0:T(8,128)(2,1)}, s32[128,128]{1,0:T(8,128)}) custom-call(s32[1]{0:T(128)S(6)} %copy.9.len_ref, s32[1,64]{1,0:T(1,128)} %bitcast.11, s32[16,128]{1,0:T(8,128)} %bitcast.10, bf16[512,512]{1,0:T(8,128)(2,1)} %bitcast.7, bf16[512,512]{1,0:T(8,128)(2,1)} %bitcast.8, bf16[512,512]{1,0:T(8,128)(2,1)} %bitcast.9, ...), custom_call_target="tpu_custom_call" | custom-call | tf_op jit(solution)/shard_map/pallas_call | solution.py:406
  57.8 9.4 %shard_map.83 = f32[128,8192]{1,0:T(8,128)} custom-call(s32[128,128]{1,0:T(8,128)} %get-tuple-element.7.ids_ref, bf16[4096,128]{1,0:T(8,128)(2,1)} %bitcast.6), custom_call_target="tpu_custom_call" | custom-call | tf_op jit(solution)/shard_map/pallas_call | solution.py:453
